TPU v7x, 32 devices: a whole 2x2x4 slice. The times are simulated.
32 devices in a mesh: dp: 8 (over z, y), tensor: 4 (over x, core).
Axes of the slice: x: 2, y: 2, z: 4, core: 2. Of those that a mesh axis runs over, the one named last changes fastest.
Arguments:
- tokens: bfloat16 [4096, 2048], P(('dp', 'tensor')), may hold values from -6 to 6
- lengths: int32 [8, 4], P('dp'), may hold values from 0 to 512, as said below
- w_query: bfloat16 [2048, 2048], P(None, 'tensor'), may hold values from -0.125 to 0.125
- w_key: bfloat16 [2048, 2048], P(None, 'tensor'), may hold values from -0.125 to 0.125
- w_value: bfloat16 [2048, 2048], P(None, 'tensor'), may hold values from -0.125 to 0.125
- w_out: bfloat16 [2048, 2048], P('tensor'), may hold values from -0.125 to 0.125
- w_gate: bfloat16 [2048, 8192], P(None, 'tensor'), may hold values from -0.125 to 0.125
- w_up: bfloat16 [2048, 8192], P(None, 'tensor'), may hold values from -0.125 to 0.125
- w_down: bfloat16 [8192, 2048], P('tensor'), may hold values from -0.0625 to 0.0625
- gain_query: float32 [2048], P('tensor'), may hold values from 0.1 to 1.9
- gain_key: float32 [2048], P('tensor'), may hold values from 0.1 to 1.9
- gain_attn: float32 [2048], replicated, may hold values from 0.1 to 1.9
- gain_mlp: float32 [2048], replicated, may hold values from 0.1 to 1.9
- cotangent: bfloat16 [4096, 2048], P(('dp', 'tensor')), may hold values from -6 to 6
Outputs:
- output: bfloat16 [4096, 2048], P(('dp', 'tensor'))
- grad_tokens: bfloat16 [4096, 2048], P(('dp', 'tensor'))
- grad_w_query: float32 [2048, 2048], P('dp', 'tensor')
- grad_w_key: float32 [2048, 2048], P('dp', 'tensor')
- grad_w_value: float32 [2048, 2048], P('dp', 'tensor')
- grad_w_out: float32 [2048, 2048], P('tensor', 'dp')
- grad_w_gate: float32 [2048, 8192], P('dp', 'tensor')
- grad_w_up: float32 [2048, 8192], P('dp', 'tensor')
- grad_w_down: float32 [8192, 2048], P('tensor', 'dp')
- grad_gain_query: float32 [2048], P('tensor')
- grad_gain_key: float32 [2048], P('tensor')
- grad_gain_attn: float32 [2048], replicated
- grad_gain_mlp: float32 [2048], replicated
Inputs may be any that keep to these rules, and one draw needn't show every extreme that they name: Each row lists the lengths of its sequences in order, then zeros; every nonzero length is 128 or more and they sum to 512; row 0 holds one sequence of 512 tokens.
All inputs are finite; a program needn't handle non-finite values.
Results may differ from a plain program's by a relative error of at most 0.023.
Values may be sent and summed in bfloat16 or wider, within the bound.
A program may use at most 256 MiB of HBM per device.

v0:
```python
import math
import jax
import jax.numpy as jnp
from jax import lax
from jax.sharding import PartitionSpec as P

HD = 128
ROW_LEN = 512
EPS = 1e-06
THETA = 500000.0


def rotate(values, offsets, rot_sign):
    half_width = values.shape[-1] // 2
    frequency = jnp.exp(
        jnp.arange(half_width, dtype=jnp.float32) * (-2.0 * math.log(THETA) / values.shape[-1])
    )
    angles = offsets.astype(jnp.float32)[..., None, None] * frequency
    cosines = jnp.cos(angles)
    sine_part = rot_sign * jnp.sin(angles)
    first_half = values[..., :half_width]
    second_half = values[..., half_width:]
    return jnp.concatenate(
        [
            first_half * cosines - second_half * sine_part,
            second_half * cosines + first_half * sine_part,
        ],
        axis=-1,
    )


def row_layout(lengths_row):
    slots = jnp.arange(lengths_row.shape[0], dtype=jnp.int32)
    seq_ends = jnp.sum(jnp.where(slots[None, :] <= slots[:, None], lengths_row[None, :], 0), axis=1)
    position = jnp.arange(ROW_LEN, dtype=jnp.int32)
    passed = (position[:, None] >= seq_ends[None, :]).astype(jnp.int32)
    segment = jnp.sum(passed, axis=1)
    seq_start = jnp.sum(passed * lengths_row[None, :], axis=1)
    return (segment, position - seq_start)


def allowed_mask(segment):
    position = jnp.arange(segment.shape[0], dtype=jnp.int32)
    return (segment[:, None] == segment[None, :]) & (position[None, :] <= position[:, None])


def times_t(left_mat, right_mat):
    return lax.dot_general(
        left_mat, right_mat, (((1,), (1,)), ((), ())), preferred_element_type=jnp.float32
    )


def t_times(left_mat, right_mat):
    return lax.dot_general(
        left_mat, right_mat, (((0,), (0,)), ((), ())), preferred_element_type=jnp.float32
    )


def masked_scores(queries_low, keys_low, segment):
    scale_factor = 1.0 / math.sqrt(queries_low.shape[-1])
    scores = (
        jnp.einsum("qhd,khd->hqk", queries_low, keys_low, preferred_element_type=jnp.float32)
        * scale_factor
    )
    return jnp.where(allowed_mask(segment)[None], scores, -1e30)


def attend(block_item):
    queries_low, keys_low, values_low, segment = block_item
    scores = masked_scores(queries_low, keys_low, segment)
    row_max = jnp.max(scores, axis=-1, keepdims=True)
    shifted = jnp.exp(scores - row_max)
    row_total = jnp.sum(shifted, axis=-1, keepdims=True)
    attn_weights = (shifted / row_total).astype(jnp.bfloat16)
    mixed = jnp.einsum("hqk,khd->qhd", attn_weights, values_low, preferred_element_type=jnp.float32)
    return (mixed.astype(jnp.bfloat16), (row_max + jnp.log(row_total))[..., 0])


def attend_back(block_item):
    queries_low, keys_low, values_low, segment, log_total, grad_mixed = block_item
    scale_factor = 1.0 / math.sqrt(queries_low.shape[-1])
    scores = masked_scores(queries_low, keys_low, segment)
    attn_weights = jnp.exp(scores - log_total[..., None])
    grad_weights = jnp.einsum(
        "qhd,khd->hqk", grad_mixed, values_low, preferred_element_type=jnp.float32
    )
    row_dots = jnp.sum(attn_weights * grad_weights, axis=-1, keepdims=True)
    grad_scores = (attn_weights * (grad_weights - row_dots)).astype(jnp.bfloat16)
    grad_queries = scale_factor * jnp.einsum(
        "hqk,khd->qhd", grad_scores, keys_low, preferred_element_type=jnp.float32
    )
    grad_keys = scale_factor * jnp.einsum(
        "hqk,qhd->khd", grad_scores, queries_low, preferred_element_type=jnp.float32
    )
    grad_values = jnp.einsum(
        "hqk,qhd->khd",
        attn_weights.astype(jnp.bfloat16),
        grad_mixed,
        preferred_element_type=jnp.float32,
    )
    return (grad_queries, grad_keys, grad_values.astype(jnp.bfloat16))


def post_norm_back(grad_in, unit_rows, inv_scale, gain_vec):
    scaled = grad_in * gain_vec
    mean_dots = jnp.mean(scaled * unit_rows, axis=-1, keepdims=True)
    return (inv_scale * (scaled - unit_rows * mean_dots), jnp.sum(grad_in * unit_rows, axis=0))


OUTER = 4


def swap(value, shift):
    size = lax.axis_size("dp")
    return lax.ppermute(value, "dp", [(d, d ^ shift) for d in range(size)])


def pick(parts, index):
    return lax.dynamic_index_in_dim(parts, index, 0, keepdims=False)


def sum_inner(parts):
    inner = parts.shape[0]
    mine = lax.axis_index("dp") % inner
    total = pick(parts, mine)
    for k in range(1, inner):
        sent = pick(parts, mine ^ k).astype(jnp.bfloat16)
        total = total + swap(sent, k).astype(jnp.float32)
    return total


def trade_outer(parts, inner):
    mine = lax.axis_index("dp") // inner
    got = [(mine, pick(parts, mine))]
    for k in range(1, OUTER):
        got.append((mine ^ k, swap(pick(parts, mine ^ k), k * inner)))
    return got


def split_rows(grad, inner):
    cols = grad.shape[1]
    return grad.reshape(OUTER, inner, -1, cols).transpose(1, 0, 2, 3)


def split_cols(grad, inner):
    rows = grad.shape[0]
    return grad.reshape(rows, OUTER, inner, -1).transpose(2, 1, 0, 3)


def scatter_sum(parts, inner):
    half = sum_inner(parts).astype(jnp.bfloat16)
    got = trade_outer(half, inner)
    return sum((g.astype(jnp.float32) for _, g in got))


def scatter_join(parts, inner, axis):
    half = sum_inner(parts).astype(jnp.bfloat16)
    got = trade_outer(half, inner)
    stack = jnp.zeros((OUTER, *got[0][1].shape), jnp.bfloat16)
    for place, block in got:
        stack = lax.dynamic_update_index_in_dim(stack, block, place, 0)
    joined = jnp.concatenate([stack[z] for z in range(OUTER)], axis=axis)
    return joined.astype(jnp.float32)


def body(
    tokens,
    lengths,
    w_query,
    w_key,
    w_value,
    w_out,
    w_gate,
    w_up,
    w_down,
    gain_query,
    gain_key,
    gain_attn,
    gain_mlp,
    cotangent,
):
    rows_dev = lengths.shape[0]
    model_width = w_query.shape[0]
    local_width = w_query.shape[1]
    head_count = local_width // HD
    gathered = lax.all_gather(tokens, "tensor", axis=0, tiled=True)
    row_count = gathered.shape[0]
    segment, offsets = jax.vmap(row_layout)(lengths)
    queries = jnp.dot(gathered, w_query, preferred_element_type=jnp.float32)
    keys_raw = jnp.dot(gathered, w_key, preferred_element_type=jnp.float32)
    values_low = jnp.dot(gathered, w_value, preferred_element_type=jnp.float32).astype(jnp.bfloat16)
    q_total, k_total = lax.psum(
        (jnp.sum(queries * queries, axis=1), jnp.sum(keys_raw * keys_raw, axis=1)), "tensor"
    )
    q_inv = lax.rsqrt(q_total / model_width + EPS)[:, None]
    k_inv = lax.rsqrt(k_total / model_width + EPS)[:, None]
    q_unit = queries * q_inv
    k_unit = keys_raw * k_inv

    def to_heads(values):
        return values.reshape(rows_dev, ROW_LEN, head_count, HD)

    queries_low = rotate(to_heads(q_unit * gain_query), offsets, 1.0).astype(jnp.bfloat16)
    keys_low = rotate(to_heads(k_unit * gain_key), offsets, 1.0).astype(jnp.bfloat16)
    values_heads = to_heads(values_low)
    mixed_heads, log_total = jax.vmap(lambda *a: attend(a))(
        queries_low, keys_low, values_heads, segment
    )
    mixed_low = mixed_heads.reshape(row_count, local_width)
    attn_out = lax.psum_scatter(
        jnp.dot(mixed_low, w_out, preferred_element_type=jnp.float32).astype(jnp.bfloat16),
        "tensor",
        scatter_dimension=0,
        tiled=True,
    ).astype(jnp.float32)
    a_inv = lax.rsqrt(jnp.mean(attn_out * attn_out, axis=1, keepdims=True) + EPS)
    a_unit = attn_out * a_inv
    hidden = tokens.astype(jnp.float32) + a_unit * gain_attn
    hidden_low = hidden.astype(jnp.bfloat16)
    hidden_all = lax.all_gather(hidden_low, "tensor", axis=0, tiled=True)
    inner_count = lax.axis_size("dp") // OUTER
    outer_index = lax.axis_index("dp") // inner_count

    def gather_group(shard):
        groups = [[z * inner_count + i for z in range(OUTER)] for i in range(inner_count)]
        part = lax.all_gather(shard, "dp", axis=0, tiled=True, axis_index_groups=groups)
        return lax.all_gather(part, "tensor", axis=0, tiled=True)

    hidden_group = gather_group(hidden_low)
    gate_acts = jnp.dot(hidden_all, w_gate, preferred_element_type=jnp.float32)
    up_acts = jnp.dot(hidden_all, w_up, preferred_element_type=jnp.float32)
    gate_sigmoid = jax.nn.sigmoid(gate_acts)
    inner_low = (gate_acts * gate_sigmoid * up_acts).astype(jnp.bfloat16)
    mlp_out = lax.psum_scatter(
        jnp.dot(inner_low, w_down, preferred_element_type=jnp.float32).astype(jnp.bfloat16),
        "tensor",
        scatter_dimension=0,
        tiled=True,
    ).astype(jnp.float32)
    f_inv = lax.rsqrt(jnp.mean(mlp_out * mlp_out, axis=1, keepdims=True) + EPS)
    f_unit = mlp_out * f_inv
    output = (hidden + f_unit * gain_mlp).astype(jnp.bfloat16)
    grad_output = cotangent.astype(jnp.float32)
    grad_mlp, grad_gain_mlp_part = post_norm_back(grad_output, f_unit, f_inv, gain_mlp)
    grad_mlp_low = grad_mlp.astype(jnp.bfloat16)
    mlp_grad_all = lax.all_gather(grad_mlp_low, "tensor", axis=0, tiled=True)
    mlp_grad_group = gather_group(grad_mlp_low)
    grad_inner = times_t(mlp_grad_all, w_down)
    grad_gate_low = (
        grad_inner * up_acts * gate_sigmoid * (1.0 + gate_acts * (1.0 - gate_sigmoid))
    ).astype(jnp.bfloat16)
    grad_up_low = (grad_inner * gate_acts * gate_sigmoid).astype(jnp.bfloat16)
    part_width = w_gate.shape[1] // OUTER
    gate_part = lax.dynamic_slice_in_dim(w_gate, outer_index * part_width, part_width, 1)
    up_part = lax.dynamic_slice_in_dim(w_up, outer_index * part_width, part_width, 1)
    down_part = lax.dynamic_slice_in_dim(w_down, outer_index * part_width, part_width, 0)
    gate_g = jnp.dot(hidden_group, gate_part, preferred_element_type=jnp.float32)
    up_g = jnp.dot(hidden_group, up_part, preferred_element_type=jnp.float32)
    sig_g = jax.nn.sigmoid(gate_g)
    inner_g = (gate_g * sig_g * up_g).astype(jnp.bfloat16)
    grad_inner_g = times_t(mlp_grad_group, down_part)
    grad_gate_g = (grad_inner_g * up_g * sig_g * (1.0 + gate_g * (1.0 - sig_g))).astype(
        jnp.bfloat16
    )
    grad_up_g = (grad_inner_g * gate_g * sig_g).astype(jnp.bfloat16)
    sum_down = scatter_join(
        split_cols(t_times(inner_g, mlp_grad_group), inner_count), inner_count, 0
    )
    sum_gate = scatter_join(
        split_rows(t_times(hidden_group, grad_gate_g), inner_count), inner_count, 1
    )
    sum_up = scatter_join(split_rows(t_times(hidden_group, grad_up_g), inner_count), inner_count, 1)
    grad_hidden = grad_output + lax.psum_scatter(
        (times_t(grad_gate_low, w_gate) + times_t(grad_up_low, w_up)).astype(jnp.bfloat16),
        "tensor",
        scatter_dimension=0,
        tiled=True,
    ).astype(jnp.float32)
    grad_attn, grad_gain_attn_part = post_norm_back(grad_hidden, a_unit, a_inv, gain_attn)
    attn_grad_all = lax.all_gather(grad_attn.astype(jnp.bfloat16), "tensor", axis=0, tiled=True)
    grad_w_out = t_times(mixed_low, attn_grad_all)
    grad_mixed = times_t(attn_grad_all, w_out).astype(jnp.bfloat16)
    grad_q_rot, grad_k_rot, grad_values_low = jax.vmap(lambda *a: attend_back(a))(
        queries_low, keys_low, values_heads, segment, log_total, to_heads(grad_mixed)
    )
    grad_q_norm = rotate(grad_q_rot, offsets, -1.0).reshape(row_count, local_width)
    grad_k_norm = rotate(grad_k_rot, offsets, -1.0).reshape(row_count, local_width)
    grad_gain_query_part = jnp.sum(grad_q_norm * q_unit, axis=0)
    grad_gain_key_part = jnp.sum(grad_k_norm * k_unit, axis=0)
    q_scaled = grad_q_norm * gain_query
    k_scaled = grad_k_norm * gain_key
    q_dots, k_dots = lax.psum(
        (jnp.sum(q_scaled * q_unit, axis=1), jnp.sum(k_scaled * k_unit, axis=1)), "tensor"
    )
    grad_queries_low = (q_inv * (q_scaled - q_unit * (q_dots / model_width)[:, None])).astype(
        jnp.bfloat16
    )
    grad_keys_low = (k_inv * (k_scaled - k_unit * (k_dots / model_width)[:, None])).astype(
        jnp.bfloat16
    )
    grad_values_flat = grad_values_low.reshape(row_count, local_width)
    grad_w_query = t_times(gathered, grad_queries_low)
    grad_w_key = t_times(gathered, grad_keys_low)
    grad_w_value = t_times(gathered, grad_values_flat)
    grad_tokens = (
        grad_hidden
        + lax.psum_scatter(
            (
                times_t(grad_queries_low, w_query)
                + times_t(grad_keys_low, w_key)
                + times_t(grad_values_flat, w_value)
            ).astype(jnp.bfloat16),
            "tensor",
            scatter_dimension=0,
            tiled=True,
        ).astype(jnp.float32)
    ).astype(jnp.bfloat16)
    tensor_start = lax.axis_index("tensor") * local_width
    zero_row = jnp.zeros((model_width,), jnp.float32)
    q_full = lax.dynamic_update_slice(zero_row, grad_gain_query_part, (tensor_start,))
    k_full = lax.dynamic_update_slice(zero_row, grad_gain_key_part, (tensor_start,))
    gain_stack = jnp.stack([q_full, k_full, grad_gain_attn_part, grad_gain_mlp_part])
    gain_total = lax.psum(gain_stack, ("dp", "tensor"))
    grad_gain_query = lax.dynamic_slice(gain_total[0], (tensor_start,), (local_width,))
    grad_gain_key = lax.dynamic_slice(gain_total[1], (tensor_start,), (local_width,))
    summed = (
        scatter_sum(split_rows(grad_w_query, inner_count), inner_count),
        scatter_sum(split_rows(grad_w_key, inner_count), inner_count),
        scatter_sum(split_rows(grad_w_value, inner_count), inner_count),
        scatter_sum(split_cols(grad_w_out, inner_count), inner_count),
        sum_gate,
        sum_up,
        sum_down,
    )
    return (
        output,
        grad_tokens,
        summed[0],
        summed[1],
        summed[2],
        summed[3],
        summed[4],
        summed[5],
        summed[6],
        grad_gain_query,
        grad_gain_key,
        gain_total[2],
        gain_total[3],
    )


def solution(mesh):
    placed = (
        P(("dp", "tensor"), None),
        P("dp", None),
        P(None, "tensor"),
        P(None, "tensor"),
        P(None, "tensor"),
        P("tensor", None),
        P(None, "tensor"),
        P(None, "tensor"),
        P("tensor", None),
        P("tensor"),
        P("tensor"),
        P(),
        P(),
        P(("dp", "tensor"), None),
    )
    return jax.shard_map(
        body,
        mesh=mesh,
        in_specs=placed,
        out_specs=(
            P(("dp", "tensor"), None),
            P(("dp", "tensor"), None),
            P("dp", "tensor"),
            P("dp", "tensor"),
            P("dp", "tensor"),
            P("tensor", "dp"),
            P("dp", "tensor"),
            P("dp", "tensor"),
            P("tensor", "dp"),
            P("tensor"),
            P("tensor"),
            P(),
            P(),
        ),
        check_vma=False,
    )
```

profile of v0, /device:TPU:9, one launch (start us, length us, event | category | flops | bytes accessed | tf_op | source)
XLA Modules:
  0.0 888.0 jit_solution(406805340475882868)
XLA Ops:
  12.2 21.6 %all-gather.9.cloned.1.call-done = bf16[512,2048]{1,0:T(8,128)(2,1)} async-done(((bf16[128,2048]{1,0:T(8,128)(2,1)}), bf16[512,2048]{1,0:T(8,128)(2,1)}) %all-gather.9.cloned.1.call-update) | async-done | bytes 2097168 | tf_op jit(solution)/shard_map/all_gather | solution.py:186
  70.3 32.8 %reduce-scatter.5.cloned.1.call-done = bf16[128,2048]{1,0:T(8,128)(2,1)} async-done(((bf16[512,2048]{1,0:T(8,128)(2,1)}), bf16[128,2048]{1,0:T(8,128)(2,1)}) %reduce-scatter.5.cloned.1.call-update) | async-done | bytes 524304 | tf_op jit(solution)/shard_map/reduce_scatter | solution.py:210
  106.8 22.8 %all-gather.11.cloned.1.call-done = bf16[512,2048]{1,0:T(8,128)(2,1)} async-done(((bf16[128,2048]{1,0:T(8,128)(2,1)}), bf16[512,2048]{1,0:T(8,128)(2,1)}) %all-gather.11.cloned.1.call-update) | async-done | bytes 2097168 | tf_op jit(solution)/shard_map/all_gather | solution.py:220
  129.6 8.6 fusion.92
  138.2 8.4 fusion.93
  148.6 9.5 %convolution_convert_fusion = bf16[512,2048]{1,0:T(8,128)(2,1)} fusion(bf16[2048,2048]{1,0:T(8,128)(2,1)} %param.22, f32[512,2048]{1,0:T(8,128)S(1)} %fusion.93, f32[512,2048]{1,0:T(8,128)S(1)} %fusion.92), kind=kOutput, calls=%fused_computation.21 | convolution fusion | flops 4302307328 | bytes 18874368 | tf_op jit(solution)/shard_map/dot_general | solution.py:235
  158.2 31.1 %reduce-scatter.7.cloned.1.call-done = bf16[128,2048]{1,0:T(8,128)(2,1)} async-done(((bf16[512,2048]{1,0:T(8,128)(2,1)}), bf16[128,2048]{1,0:T(8,128)(2,1)}) %reduce-scatter.7.cloned.1.call-update) | async-done | bytes 524304 | tf_op jit(solution)/shard_map/reduce_scatter | solution.py:234
  194.3 23.1 %all-gather.13.cloned.1.call-done = bf16[512,2048]{1,0:T(8,128)(2,1)} async-done(((bf16[128,2048]{1,0:T(8,128)(2,1)}), bf16[512,2048]{1,0:T(8,128)(2,1)}) %all-gather.13.cloned.1.call-update) | async-done | bytes 2097168 | tf_op jit(solution)/shard_map/all_gather | solution.py:246
  225.0 13.6 %fusion.25 = f32[512,2048]{1,0:T(8,128)} fusion(bf16[2048,2048]{1,0:T(8,128)(2,1)} %param.20, f32[512,2048]{1,0:T(8,128)} %copy-done.53, f32[512,2048]{1,0:T(8,128)S(1)} %fusion.94, f32[512,2048]{1,0:T(8,128)} %copy-done.54), kind=kOutput, calls=%fused_computation.56 | convolution fusion | flops 4305453056 | bytes 25165824 | tf_op jit(solution)/shard_map/dot_general | solution.py:48
  238.6 11.8 %add_convert_fusion.1 = bf16[512,2048]{1,0:T(8,128)(2,1)} fusion(f32[512,2048]{1,0:T(8,128)} %fusion.25, bf16[2048,2048]{1,0:T(8,128)(2,1)} %param.21, f32[512,2048]{1,0:T(8,128)S(1)} %fusion.94, f32[512,2048]{1,0:T(8,128)} %copy-done.53), kind=kOutput, calls=%fused_computation.8 | convolution fusion | flops 4303355904 | bytes 23068672 | tf_op jit(solution)/shard_map/dot_general | solution.py:48
  251.3 30.4 %reduce-scatter.9.cloned.1.call-done = bf16[128,2048]{1,0:T(8,128)(2,1)} async-done(((bf16[512,2048]{1,0:T(8,128)(2,1)}), bf16[128,2048]{1,0:T(8,128)(2,1)}) %reduce-scatter.9.cloned.1.call-update) | async-done | bytes 524304 | tf_op jit(solution)/shard_map/reduce_scatter | solution.py:273
  286.9 41.1 %all-gather.17.cloned.1.call-done = bf16[512,2048]{1,0:T(8,128)(2,1)} async-done(((bf16[128,2048]{1,0:T(8,128)(2,1)}), bf16[512,2048]{1,0:T(8,128)(2,1)}) %all-gather.17.cloned.1.call-update) | async-done | bytes 2097168 | tf_op jit(solution)/shard_map/all_gather | solution.py:226
  328.2 25.5 %all-gather.15.cloned.1.call-done = bf16[512,2048]{1,0:T(8,128)(2,1)} async-done(((bf16[128,2048]{1,0:T(8,128)(2,1)}), bf16[512,2048]{1,0:T(8,128)(2,1)}) %all-gather.15.cloned.1.call-update) | async-done | bytes 2097168 | tf_op jit(solution)/shard_map/all_gather | solution.py:280
  399.8 60.7 %all-gather.19.cloned.1.call-done = bf16[2048,2048]{1,0:T(8,128)(2,1)} async-done(((bf16[512,2048]{1,0:T(8,128)(2,1)}), bf16[2048,2048]{1,0:T(8,128)(2,1)}) %all-gather.19.cloned.1.call-update) | async-done | bytes 8388624 | tf_op jit(solution)/shard_map/all_gather | solution.py:227
  460.5 10.6 %fusion.14 = f32[2048,512]{1,0:T(8,128)} fusion(bf16[2048,2048]{1,0:T(8,128)(2,1)} %all-gather.19.cloned.1.call-done, bf16[2048,2048]{1,0:T(8,128)(2,1)} %param.20, s32[]{:T(128)S(6)} %select_n.141), kind=kOutput, calls=%fused_computation.44 | convolution fusion | flops 4294967296 | bytes 14680068 | tf_op jit(solution)/shard_map/dot_general | solution.py:257
  471.2 8.7 fusion.18
  554.8 71.2 %psum.39 = f32[4,2048]{1,0:T(4,128)S(1)} all-reduce(f32[4,2048]{1,0:T(4,128)S(1)} %pad_maximum_fusion.8), channel_id=1, replica_groups=mesh['dp'=8,'tensor'=4] {'dp','tensor'}, use_global_device_ids=true, to_apply=%region_26.27 | all-reduce | flops 8192 | bytes 65536 | tf_op jit(solution)/shard_map/psum | solution.py:323
  668.2 14.5 %collective-permute-done.2 = bf16[256,512]{1,0:T(8,128)(2,1)S(1)} collective-permute-done((bf16[256,512]{1,0:T(8,128)(2,1)S(1)}, bf16[256,512]{1,0:T(8,128)(2,1)S(1)}, u32[]{:S(2)}, u32[]{:S(2)}) %collective-permute-start.2) | collective-permute-done | bytes 262176 | tf_op jit(solution)/shard_map/ppermute | solution.py:115
  688.4 13.6 %collective-permute-done.7 = bf16[256,512]{1,0:T(8,128)(2,1)S(1)} collective-permute-done((bf16[256,512]{1,0:T(8,128)(2,1)S(1)}, bf16[256,512]{1,0:T(8,128)(2,1)S(1)}, u32[]{:S(2)}, u32[]{:S(2)}) %collective-permute-start.7) | collective-permute-done | bytes 262176 | tf_op jit(solution)/shard_map/ppermute | solution.py:115
  710.9 13.6 %collective-permute-done.11 = bf16[256,512]{1,0:T(8,128)(2,1)S(1)} collective-permute-done((bf16[256,512]{1,0:T(8,128)(2,1)S(1)}, bf16[256,512]{1,0:T(8,128)(2,1)S(1)}, u32[]{:S(2)}, u32[]{:S(2)}) %collective-permute-start.11) | collective-permute-done | bytes 262176 | tf_op jit(solution)/shard_map/ppermute | solution.py:115
  772.6 9.7 %fusion.5 = f32[512,2048]{1,0:T(8,128)} fusion(bf16[2048,2048]{1,0:T(8,128)(2,1)S(1)} %bitcast.317, f32[2048,512]{1,0:T(8,128)} %fusion.18, f32[2048,512]{1,0:T(8,128)} %fusion.14), kind=kOutput, calls=%fused_computation.25 | convolution fusion | flops 4301258752 | bytes 20971520 | tf_op jit(solution)/shard_map/dot_general | solution.py:54
  807.9 18.9 %collective-permute-done.24 = bf16[4,512,256]{2,1,0:T(8,128)(2,1)S(1)} collective-permute-done((bf16[4,512,256]{2,1,0:T(8,128)(2,1)S(1)}, bf16[4,512,256]{2,1,0:T(8,128)(2,1)S(1)}, u32[]{:S(2)}, u32[]{:S(2)}) %collective-permute-start.24) | collective-permute-done | bytes 1048608 | tf_op jit(solution)/shard_map/ppermute | solution.py:115
  834.6 14.9 %collective-permute-done.22 = bf16[256,512]{1,0:T(8,128)(2,1)S(1)} collective-permute-done((bf16[256,512]{1,0:T(8,128)(2,1)S(1)}, bf16[256,512]{1,0:T(8,128)(2,1)S(1)}, u32[]{:S(2)}, u32[]{:S(2)}) %collective-permute-start.22) | collective-permute-done | bytes 262176 | tf_op jit(solution)/shard_map/ppermute | solution.py:115
  849.5 15.1 %collective-permute-done.23 = bf16[256,512]{1,0:T(8,128)(2,1)S(1)} collective-permute-done((bf16[256,512]{1,0:T(8,128)(2,1)S(1)}, bf16[256,512]{1,0:T(8,128)(2,1)S(1)}, u32[]{:S(2)}, u32[]{:S(2)}) %collective-permute-start.23) | collective-permute-done | bytes 262176 | tf_op jit(solution)/shard_map/ppermute | solution.py:115
  (334 shorter events, 340.4 us)
Async XLA Ops:
  7.9 95.1 %reduce-scatter.5.cloned.1.call-start = ((), (), s32[]{:S(2)}) async-start(), calls=%async_computation.5 | async-start | bytes 2621440 | tf_op jit(solution)/shard_map/reduce_scatter | solution.py:210
  70.2 59.4 %all-gather.11.cloned.1.call-start = ((), (), s32[]{:S(2)}) async-start(), calls=%async_computation.6 | async-start | bytes 2621440 | tf_op jit(solution)/shard_map/all_gather | solution.py:220
  106.4 82.9 %reduce-scatter.7.cloned.1.call-start = ((), (), s32[]{:S(2)}) async-start(), calls=%async_computation.7 | async-start | bytes 2621440 | tf_op jit(solution)/shard_map/reduce_scatter | solution.py:234
  158.1 59.3 %all-gather.13.cloned.1.call-start = ((), (), s32[]{:S(2)}) async-start(), calls=%async_computation.8 | async-start | bytes 2621440 | tf_op jit(solution)/shard_map/all_gather | solution.py:246
  194.2 87.4 %reduce-scatter.9.cloned.1.call-start = ((), (), s32[]{:S(2)}) async-start(), calls=%async_computation.9 | async-start | bytes 2621440 | tf_op jit(solution)/shard_map/reduce_scatter | solution.py:273
  250.5 77.5 %all-gather.17.cloned.1.call-start = ((), (), s32[]{:S(2)}) async-start(), calls=%async_computation.12 | async-start | bytes 2621440 | tf_op jit(solution)/shard_map/all_gather | solution.py:226
  251.2 102.6 %all-gather.15.cloned.1.call-start = ((), (), s32[]{:S(2)}) async-start(), calls=%async_computation.10 | async-start | bytes 2621440 | tf_op jit(solution)/shard_map/all_gather | solution.py:280
  286.1 113.6 %all-gather.21.cloned.1.call-start = ((), (), s32[]{:S(2)}) async-start(), calls=%async_computation.14 | async-start | bytes 2621440 | tf_op jit(solution)/shard_map/all_gather | solution.py:226
  286.9 173.7 %all-gather.19.cloned.1.call-start = ((), (), s32[]{:S(2)}) async-start(), calls=%async_computation.13 | async-start | bytes 10485760 | tf_op jit(solution)/shard_map/all_gather | solution.py:227
  328.0 412.5 %reduce-scatter.11.cloned.1.call-start = ((), (), s32[]{:S(2)}) async-start(), calls=%async_computation.11 | async-start | bytes 2621440 | tf_op jit(solution)/shard_map/reduce_scatter | solution.py:307
  395.6 347.0 %all-gather.23.cloned.1.call-start = ((), (), s32[]{:S(2)}) async-start(), calls=%async_computation.15 | async-start | bytes 10485760 | tf_op jit(solution)/shard_map/all_gather | solution.py:227
  500.9 147.4 %collective-permute-start = (bf16[4,256,512]{2,1,0:T(8,128)(2,1)}, bf16[4,256,512]{2,1,0:T(8,128)(2,1)}, u32[]{:S(2)}, u32[]{:S(2)}) collective-permute-start(bf16[4,256,512]{2,1,0:T(8,128)(2,1)} %bitcast.298), channel_id=1, source_target_pairs={{0,4},{4,0},{8,12},{12,8},{16,20},{20,16},{24,28},{28,24},{1,5},{5... | collective-permute-start | bytes 3145736 | tf_op jit(solution)/shard_map/ppermute | solution.py:115
  523.5 130.4 %collective-permute-start.4 = (bf16[4,256,512]{2,1,0:T(8,128)(2,1)}, bf16[4,256,512]{2,1,0:T(8,128)(2,1)}, u32[]{:S(2)}, u32[]{:S(2)}) collective-permute-start(bf16[4,256,512]{2,1,0:T(8,128)(2,1)} %bitcast.297), channel_id=1, source_target_pairs={{0,4},{4,0},{8,12},{12,8},{16,20},{20,16},{24,28},{28,24},{1,5},{5... | collective-permute-start | bytes 3145736 | tf_op jit(solution)/shard_map/ppermute | solution.py:115
  542.2 113.6 %collective-permute-start.8 = (bf16[4,256,512]{2,1,0:T(8,128)(2,1)}, bf16[4,256,512]{2,1,0:T(8,128)(2,1)}, u32[]{:S(2)}, u32[]{:S(2)}) collective-permute-start(bf16[4,256,512]{2,1,0:T(8,128)(2,1)} %bitcast.296), channel_id=1, source_target_pairs={{0,4},{4,0},{8,12},{12,8},{16,20},{20,16},{24,28},{28,24},{1,5},{5... | collective-permute-start | bytes 3145736 | tf_op jit(solution)/shard_map/ppermute | solution.py:115
  548.5 109.2 %collective-permute-start.12 = (bf16[4,512,256]{2,1,0:T(8,128)(2,1)}, bf16[4,512,256]{2,1,0:T(8,128)(2,1)}, u32[]{:S(2)}, u32[]{:S(2)}) collective-permute-start(bf16[4,512,256]{2,1,0:T(8,128)(2,1)} %fusion.56), channel_id=1, source_target_pairs={{0,4},{4,0},{8,12},{12,8},{16,20},{20,16},{24,28},{28,24},{1,5},{5... | collective-permute-start | bytes 3145736 | tf_op jit(solution)/shard_map/ppermute | solution.py:115
  655.7 46.2 %collective-permute-start.7 = (bf16[256,512]{1,0:T(8,128)(2,1)S(1)}, bf16[256,512]{1,0:T(8,128)(2,1)S(1)}, u32[]{:S(2)}, u32[]{:S(2)}) collective-permute-start(bf16[256,512]{1,0:T(8,128)(2,1)S(1)} %get-tuple-element.66), channel_id=1, source_target_pairs={{0,24},{4,28},{8,16},{12,20},{16,8},{20,12},{24,0},{28,4},{1,25},{... | collective-permute-start | bytes 786440 | tf_op jit(solution)/shard_map/ppermute | solution.py:115
  657.8 48.1 %collective-permute-start.6 = (bf16[256,512]{1,0:T(8,128)(2,1)S(1)}, bf16[256,512]{1,0:T(8,128)(2,1)S(1)}, u32[]{:S(2)}, u32[]{:S(2)}) collective-permute-start(bf16[256,512]{1,0:T(8,128)(2,1)S(1)} %get-tuple-element.67), channel_id=1, source_target_pairs={{0,16},{4,20},{8,24},{12,28},{16,0},{20,4},{24,8},{28,12},{1,17},{... | collective-permute-start | bytes 786440 | tf_op jit(solution)/shard_map/ppermute | solution.py:115
  668.2 38.7 %collective-permute-start.5 = (bf16[256,512]{1,0:T(8,128)(2,1)S(1)}, bf16[256,512]{1,0:T(8,128)(2,1)S(1)}, u32[]{:S(2)}, u32[]{:S(2)}) collective-permute-start(bf16[256,512]{1,0:T(8,128)(2,1)S(1)} %get-tuple-element.65), channel_id=1, source_target_pairs={{0,8},{4,12},{8,0},{12,4},{16,24},{20,28},{24,16},{28,20},{1,9},{5... | collective-permute-start | bytes 786440 | tf_op jit(solution)/shard_map/ppermute | solution.py:115
  682.7 41.8 %collective-permute-start.11 = (bf16[256,512]{1,0:T(8,128)(2,1)S(1)}, bf16[256,512]{1,0:T(8,128)(2,1)S(1)}, u32[]{:S(2)}, u32[]{:S(2)}) collective-permute-start(bf16[256,512]{1,0:T(8,128)(2,1)S(1)} %get-tuple-element.63), channel_id=1, source_target_pairs={{0,24},{4,28},{8,16},{12,20},{16,8},{20,12},{24,0},{28,4},{1,25},{... | collective-permute-start | bytes 786440 | tf_op jit(solution)/shard_map/ppermute | solution.py:115
  683.8 44.5 %collective-permute-start.10 = (bf16[256,512]{1,0:T(8,128)(2,1)S(1)}, bf16[256,512]{1,0:T(8,128)(2,1)S(1)}, u32[]{:S(2)}, u32[]{:S(2)}) collective-permute-start(bf16[256,512]{1,0:T(8,128)(2,1)S(1)} %get-tuple-element.64), channel_id=1, source_target_pairs={{0,16},{4,20},{8,24},{12,28},{16,0},{20,4},{24,8},{28,12},{1,17},{... | collective-permute-start | bytes 786440 | tf_op jit(solution)/shard_map/ppermute | solution.py:115
  759.2 37.0 %collective-permute-start.16 = (bf16[4,256,512]{2,1,0:T(8,128)(2,1)}, bf16[4,256,512]{2,1,0:T(8,128)(2,1)}, u32[]{:S(2)}, u32[]{:S(2)}) collective-permute-start(bf16[4,256,512]{2,1,0:T(8,128)(2,1)} %fusion.58), channel_id=1, source_target_pairs={{0,4},{4,0},{8,12},{12,8},{16,20},{20,16},{24,28},{28,24},{1,5},{5... | collective-permute-start | bytes 3145736 | tf_op jit(solution)/shard_map/ppermute | solution.py:115
  830.5 34.2 %collective-permute-start.23 = (bf16[256,512]{1,0:T(8,128)(2,1)S(1)}, bf16[256,512]{1,0:T(8,128)(2,1)S(1)}, u32[]{:S(2)}, u32[]{:S(2)}) collective-permute-start(bf16[256,512]{1,0:T(8,128)(2,1)S(1)} %get-tuple-element.47), channel_id=1, source_target_pairs={{0,24},{4,28},{8,16},{12,20},{16,8},{20,12},{24,0},{28,4},{1,25},{... | collective-permute-start | bytes 786440 | tf_op jit(solution)/shard_map/ppermute | solution.py:115
  831.9 37.3 %collective-permute-start.26 = (bf16[512,256]{1,0:T(8,128)(2,1)S(1)}, bf16[512,256]{1,0:T(8,128)(2,1)S(1)}, u32[]{:S(2)}, u32[]{:S(2)}) collective-permute-start(bf16[512,256]{1,0:T(8,128)(2,1)S(1)} %get-tuple-element.40), channel_id=1, source_target_pairs={{0,16},{4,20},{8,24},{12,28},{16,0},{20,4},{24,8},{28,12},{1,17},{... | collective-permute-start | bytes 786440 | tf_op jit(solution)/shard_map/ppermute | solution.py:115
  833.4 42.5 %collective-permute-start.27 = (bf16[512,256]{1,0:T(8,128)(2,1)S(1)}, bf16[512,256]{1,0:T(8,128)(2,1)S(1)}, u32[]{:S(2)}, u32[]{:S(2)}) collective-permute-start(bf16[512,256]{1,0:T(8,128)(2,1)S(1)} %get-tuple-element.39), channel_id=1, source_target_pairs={{0,24},{4,28},{8,16},{12,20},{16,8},{20,12},{24,0},{28,4},{1,25},{... | collective-permute-start | bytes 786440 | tf_op jit(solution)/shard_map/ppermute | solution.py:115
  (77 other events, 1092.5 us)
Sparse Core Ops, SparseCore 0:
  9.6 24.1 all-gather.8
  70.3 32.6 reduce-scatter.4
  106.5 23.0 all-gather.10
  158.2 31.0 reduce-scatter.6
  194.4 22.9 all-gather.12
  250.6 31.0 reduce-scatter.8
  283.9 44.0 all-gather.16
  330.2 23.5 all-gather.14
  356.0 43.6 all-gather.20
  401.2 59.2 all-gather.18
  463.8 30.9 reduce-scatter.10
  496.2 58.7 all-gather.22
where the time goes:
time: 898 us; the launch traced here: 888 us
  waiting for transfers between devices  420 us (47%)
  matrix products  149 us (17%)
  local copies, waits for them, and re-layouts  124 us (14%)
  blocking collectives  82.2 us (9%)
  other arithmetic  56.8 us (6%)
  starting transfers between devices  38.8 us (4%)
  between operations  15.9 us (2%)
    ppermute x28, waiting for transfers between devices, swap(): return lax.ppermute(value, 'dp', [(d, d ^ shift) for d in range(size)])  125 us
    psum x1, blocking collectives, body(): gain_total = lax.psum(gain_stack, ('dp', 'tensor'))  71.2 us
    all_gather x2, waiting for transfers between devices, gather_group(): return lax.all_gather(part, 'tensor', axis=0, tiled=True)  60.7 us
    dot_general x8, matrix products, times_t(): lax.dot_general(left_mat, right_mat, (((1,), (1,)), ((), ())), preferred_...  49.7 us
    all_gather x2, waiting for transfers between devices, gather_group(): lax.all_gather(shard, 'dp', axis=0, tiled=True, axis_index_groups=groups)  45.1 us
    another operation x12, local copies, waits for them, and re-layouts  42.2 us
    ppermute x28, starting transfers between devices, swap(): return lax.ppermute(value, 'dp', [(d, d ^ shift) for d in range(size)])  37.8 us
    dot_general x7, matrix products, t_times(): lax.dot_general(left_mat, right_mat, (((0,), (0,)), ((), ())), preferred_...  36.6 us
  transfers between devices with their start and end apart: 40, of which 24 were waited for; matrix products, arithmetic and copies ran while one was open for 23% of the time, Pallas kernels for 0%

commit v1 on v0

--- a/solution.py
+++ b/solution.py
@@ -183,7 +183,9 @@
     model_width = w_query.shape[0]
     local_width = w_query.shape[1]
     head_count = local_width // HD
-    gathered = lax.all_gather(tokens, "tensor", axis=0, tiled=True)
+    gathered = jnp.concatenate(
+        lax.all_to_all(jnp.stack([tokens] * lax.axis_size("tensor")), "tensor", 0, 0), axis=0
+    )
     row_count = gathered.shape[0]
     segment, offsets = jax.vmap(row_layout)(lengths)
     queries = jnp.dot(gathered, w_query, preferred_element_type=jnp.float32)

time: 898 us -> 902 us (level)
  starting transfers between devices: 38.8 us -> 55.7 us
  waiting for transfers between devices: 420 us -> 408 us
    all_to_all x0 -> x1, waiting for transfers between devices: none -> 22 us  [body(): lax.all_to_all(jnp.stack([tokens] * lax.axis_size('tensor')), 'tensor', 0...]
    all_gather x1 -> x0, waiting for transfers between devices: 21.6 us -> none  [body(): gathered = lax.all_gather(tokens, 'tensor', axis=0, tiled=True)]
    all_gather x1, waiting for transfers between devices: 22.8 us -> 10.7 us  [body(): hidden_all = lax.all_gather(hidden_low, 'tensor', axis=0, tiled=True)]
    reduce_scatter x1, starting transfers between devices: 0.39 us -> 12.4 us  [body(): lax.psum_scatter(jnp.dot(inner_low, w_down, preferred_element_type=jnp.fl...]
    unnamed x130 -> x128, local copies, waits for them, and re-layouts: 34.7 us -> 29.9 us
    another operation x12 -> x13, local copies, waits for them, and re-layouts: 42.2 us -> 42.4 us
where the time goes in v1:
time: 902 us; the launch traced here: 891 us
  waiting for transfers between devices  408 us (45%)
  matrix products  155 us (17%)
  local copies, waits for them, and re-layouts  120 us (13%)
  blocking collectives  82.6 us (9%)
  starting transfers between devices  55.7 us (6%)
  other arithmetic  55.5 us (6%)
  between operations  15.3 us (2%)
    ppermute x28, waiting for transfers between devices, swap(): return lax.ppermute(value, 'dp', [(d, d ^ shift) for d in range(size)])  125 us
    psum x1, blocking collectives, body(): gain_total = lax.psum(gain_stack, ('dp', 'tensor'))  70.8 us
    all_gather x2, waiting for transfers between devices, gather_group(): return lax.all_gather(part, 'tensor', axis=0, tiled=True)  60.9 us
    dot_general x8, matrix products, times_t(): lax.dot_general(left_mat, right_mat, (((1,), (1,)), ((), ())), preferred_...  49.7 us
    all_gather x2, waiting for transfers between devices, gather_group(): lax.all_gather(shard, 'dp', axis=0, tiled=True, axis_index_groups=groups)  44.8 us
    dot_general x7, matrix products, t_times(): lax.dot_general(left_mat, right_mat, (((0,), (0,)), ((), ())), preferred_...  41.3 us
    another operation x12, local copies, waits for them, and re-layouts  39.6 us
    ppermute x28, starting transfers between devices, swap(): return lax.ppermute(value, 'dp', [(d, d ^ shift) for d in range(size)])  37.6 us
  transfers between devices with their start and end apart: 40, of which 24 were waited for; matrix products, arithmetic and copies ran while one was open for 23% of the time, Pallas kernels for 0%

profile of v1, /device:TPU:9, one launch (start us, length us, event | category | flops | bytes accessed | tf_op | source)
XLA Modules:
  0.0 891.1 jit_solution(6461365099941111488)
XLA Ops:
  18.0 22.0 %all-to-all-done = bf16[4,128,2048]{2,1,0:T(8,128)(2,1)} async-done(((bf16[4,128,2048]{2,1,0:T(8,128)(2,1)}), bf16[4,128,2048]{2,1,0:T(8,128)(2,1)}, u32[]{:S(2)}, u32[]{:S(2)}) %all-to-all-start) | async-done | bytes 2097184 | tf_op jit(solution)/shard_map/all_to_all | solution.py:187
  80.0 32.5 %reduce-scatter.5.cloned.1.call-done = bf16[128,2048]{1,0:T(8,128)(2,1)} async-done(((bf16[512,2048]{1,0:T(8,128)(2,1)}), bf16[128,2048]{1,0:T(8,128)(2,1)}) %reduce-scatter.5.cloned.1.call-update) | async-done | bytes 524304 | tf_op jit(solution)/shard_map/reduce_scatter | solution.py:212
  115.8 12.4 %reduce-scatter.7.cloned.1.call-start = ((), (), s32[]{:S(2)}) async-start(), calls=%async_computation.7 | async-start | bytes 2621440 | tf_op jit(solution)/shard_map/reduce_scatter | solution.py:236
  128.2 10.7 %all-gather.8.cloned.1.call-done = bf16[512,2048]{1,0:T(8,128)(2,1)} async-done(((bf16[128,2048]{1,0:T(8,128)(2,1)}), bf16[512,2048]{1,0:T(8,128)(2,1)}) %all-gather.8.cloned.1.call-update) | async-done | bytes 2097168 | tf_op jit(solution)/shard_map/all_gather | solution.py:222
  138.9 8.6 fusion.92
  147.5 8.4 fusion.93
  163.9 31.1 %reduce-scatter.7.cloned.1.call-done = bf16[128,2048]{1,0:T(8,128)(2,1)} async-done(((bf16[512,2048]{1,0:T(8,128)(2,1)}), bf16[128,2048]{1,0:T(8,128)(2,1)}) %reduce-scatter.7.cloned.1.call-update) | async-done | bytes 524304 | tf_op jit(solution)/shard_map/reduce_scatter | solution.py:236
  200.1 23.1 %all-gather.10.cloned.1.call-done = bf16[512,2048]{1,0:T(8,128)(2,1)} async-done(((bf16[128,2048]{1,0:T(8,128)(2,1)}), bf16[512,2048]{1,0:T(8,128)(2,1)}) %all-gather.10.cloned.1.call-update) | async-done | bytes 2097168 | tf_op jit(solution)/shard_map/all_gather | solution.py:248
  230.8 13.6 %fusion.25 = f32[512,2048]{1,0:T(8,128)} fusion(bf16[2048,2048]{1,0:T(8,128)(2,1)} %param.20, f32[512,2048]{1,0:T(8,128)} %copy-done.50, f32[512,2048]{1,0:T(8,128)S(1)} %fusion.94, f32[512,2048]{1,0:T(8,128)} %copy-done.51), kind=kOutput, calls=%fused_computation.56 | convolution fusion | flops 4305453056 | bytes 25165824 | tf_op jit(solution)/shard_map/dot_general | solution.py:48
  244.5 11.8 %add_convert_fusion.1 = bf16[512,2048]{1,0:T(8,128)(2,1)} fusion(f32[512,2048]{1,0:T(8,128)} %fusion.25, bf16[2048,2048]{1,0:T(8,128)(2,1)} %param.21, f32[512,2048]{1,0:T(8,128)S(1)} %fusion.94, f32[512,2048]{1,0:T(8,128)} %copy-done.50), kind=kOutput, calls=%fused_computation.8 | convolution fusion | flops 4303355904 | bytes 23068672 | tf_op jit(solution)/shard_map/dot_general | solution.py:48
  256.9 30.6 %reduce-scatter.9.cloned.1.call-done = bf16[128,2048]{1,0:T(8,128)(2,1)} async-done(((bf16[512,2048]{1,0:T(8,128)(2,1)}), bf16[128,2048]{1,0:T(8,128)(2,1)}) %reduce-scatter.9.cloned.1.call-update) | async-done | bytes 524304 | tf_op jit(solution)/shard_map/reduce_scatter | solution.py:275
  292.7 40.9 %all-gather.14.cloned.1.call-done = bf16[512,2048]{1,0:T(8,128)(2,1)} async-done(((bf16[128,2048]{1,0:T(8,128)(2,1)}), bf16[512,2048]{1,0:T(8,128)(2,1)}) %all-gather.14.cloned.1.call-update) | async-done | bytes 2097168 | tf_op jit(solution)/shard_map/all_gather | solution.py:228
  334.0 25.5 %all-gather.12.cloned.1.call-done = bf16[512,2048]{1,0:T(8,128)(2,1)} async-done(((bf16[128,2048]{1,0:T(8,128)(2,1)}), bf16[512,2048]{1,0:T(8,128)(2,1)}) %all-gather.12.cloned.1.call-update) | async-done | bytes 2097168 | tf_op jit(solution)/shard_map/all_gather | solution.py:282
  405.5 60.9 %all-gather.16.cloned.1.call-done = bf16[2048,2048]{1,0:T(8,128)(2,1)} async-done(((bf16[512,2048]{1,0:T(8,128)(2,1)}), bf16[2048,2048]{1,0:T(8,128)(2,1)}) %all-gather.16.cloned.1.call-update) | async-done | bytes 8388624 | tf_op jit(solution)/shard_map/all_gather | solution.py:229
  466.4 10.6 %fusion.14 = f32[2048,512]{1,0:T(8,128)} fusion(bf16[2048,2048]{1,0:T(8,128)(2,1)} %all-gather.16.cloned.1.call-done, bf16[2048,2048]{1,0:T(8,128)(2,1)} %param.20, s32[]{:T(128)S(6)} %select_n.141), kind=kOutput, calls=%fused_computation.44 | convolution fusion | flops 4294967296 | bytes 14680068 | tf_op jit(solution)/shard_map/dot_general | solution.py:259
  559.1 70.8 %psum.39 = f32[4,2048]{1,0:T(4,128)S(1)} all-reduce(f32[4,2048]{1,0:T(4,128)S(1)} %pad_maximum_fusion.8), channel_id=1, replica_groups=mesh['dp'=8,'tensor'=4] {'dp','tensor'}, use_global_device_ids=true, to_apply=%region_26.27 | all-reduce | flops 8192 | bytes 65536 | tf_op jit(solution)/shard_map/psum | solution.py:325
  671.9 14.5 %collective-permute-done.2 = bf16[256,512]{1,0:T(8,128)(2,1)S(1)} collective-permute-done((bf16[256,512]{1,0:T(8,128)(2,1)S(1)}, bf16[256,512]{1,0:T(8,128)(2,1)S(1)}, u32[]{:S(2)}, u32[]{:S(2)}) %collective-permute-start.2) | collective-permute-done | bytes 262176 | tf_op jit(solution)/shard_map/ppermute | solution.py:115
  692.1 13.7 %collective-permute-done.7 = bf16[256,512]{1,0:T(8,128)(2,1)S(1)} collective-permute-done((bf16[256,512]{1,0:T(8,128)(2,1)S(1)}, bf16[256,512]{1,0:T(8,128)(2,1)S(1)}, u32[]{:S(2)}, u32[]{:S(2)}) %collective-permute-start.7) | collective-permute-done | bytes 262176 | tf_op jit(solution)/shard_map/ppermute | solution.py:115
  714.8 13.6 %collective-permute-done.11 = bf16[256,512]{1,0:T(8,128)(2,1)S(1)} collective-permute-done((bf16[256,512]{1,0:T(8,128)(2,1)S(1)}, bf16[256,512]{1,0:T(8,128)(2,1)S(1)}, u32[]{:S(2)}, u32[]{:S(2)}) %collective-permute-start.11) | collective-permute-done | bytes 262176 | tf_op jit(solution)/shard_map/ppermute | solution.py:115
  764.0 8.3 fusion.4
  776.3 9.7 %fusion.5 = f32[512,2048]{1,0:T(8,128)} fusion(bf16[2048,2048]{1,0:T(8,128)(2,1)S(1)} %bitcast.320, f32[2048,512]{1,0:T(8,128)} %fusion.18, f32[2048,512]{1,0:T(8,128)} %fusion.14), kind=kOutput, calls=%fused_computation.25 | convolution fusion | flops 4301258752 | bytes 20971520 | tf_op jit(solution)/shard_map/dot_general | solution.py:54
  811.6 18.9 %collective-permute-done.24 = bf16[4,512,256]{2,1,0:T(8,128)(2,1)S(1)} collective-permute-done((bf16[4,512,256]{2,1,0:T(8,128)(2,1)S(1)}, bf16[4,512,256]{2,1,0:T(8,128)(2,1)S(1)}, u32[]{:S(2)}, u32[]{:S(2)}) %collective-permute-start.24) | collective-permute-done | bytes 1048608 | tf_op jit(solution)/shard_map/ppermute | solution.py:115
  838.3 14.9 %collective-permute-done.22 = bf16[256,512]{1,0:T(8,128)(2,1)S(1)} collective-permute-done((bf16[256,512]{1,0:T(8,128)(2,1)S(1)}, bf16[256,512]{1,0:T(8,128)(2,1)S(1)}, u32[]{:S(2)}, u32[]{:S(2)}) %collective-permute-start.22) | collective-permute-done | bytes 262176 | tf_op jit(solution)/shard_map/ppermute | solution.py:115
  853.3 15.1 %collective-permute-done.23 = bf16[256,512]{1,0:T(8,128)(2,1)S(1)} collective-permute-done((bf16[256,512]{1,0:T(8,128)(2,1)S(1)}, bf16[256,512]{1,0:T(8,128)(2,1)S(1)}, u32[]{:S(2)}, u32[]{:S(2)}) %collective-permute-start.23) | collective-permute-done | bytes 262176 | tf_op jit(solution)/shard_map/ppermute | solution.py:115
  (333 shorter events, 353.6 us)
Async XLA Ops:
  15.0 97.4 %reduce-scatter.5.cloned.1.call-start = ((), (), s32[]{:S(2)}) async-start(), calls=%async_computation.5 | async-start | bytes 2621440 | tf_op jit(solution)/shard_map/reduce_scatter | solution.py:212
  79.9 59.0 %all-gather.8.cloned.1.call-start = ((), (), s32[]{:S(2)}) async-start(), calls=%async_computation.6 | async-start | bytes 2621440 | tf_op jit(solution)/shard_map/all_gather | solution.py:222
  115.8 79.3 %reduce-scatter.7.cloned.1.call-start = ((), (), s32[]{:S(2)}) async-start(), calls=%async_computation.7 | async-start | bytes 2621440 | tf_op jit(solution)/shard_map/reduce_scatter | solution.py:236
  163.9 59.3 %all-gather.10.cloned.1.call-start = ((), (), s32[]{:S(2)}) async-start(), calls=%async_computation.8 | async-start | bytes 2621440 | tf_op jit(solution)/shard_map/all_gather | solution.py:248
  200.1 87.4 %reduce-scatter.9.cloned.1.call-start = ((), (), s32[]{:S(2)}) async-start(), calls=%async_computation.9 | async-start | bytes 2621440 | tf_op jit(solution)/shard_map/reduce_scatter | solution.py:275
  256.3 77.4 %all-gather.14.cloned.1.call-start = ((), (), s32[]{:S(2)}) async-start(), calls=%async_computation.12 | async-start | bytes 2621440 | tf_op jit(solution)/shard_map/all_gather | solution.py:228
  256.9 102.6 %all-gather.12.cloned.1.call-start = ((), (), s32[]{:S(2)}) async-start(), calls=%async_computation.10 | async-start | bytes 2621440 | tf_op jit(solution)/shard_map/all_gather | solution.py:282
  291.9 113.5 %all-gather.18.cloned.1.call-start = ((), (), s32[]{:S(2)}) async-start(), calls=%async_computation.14 | async-start | bytes 2621440 | tf_op jit(solution)/shard_map/all_gather | solution.py:228
  292.7 173.7 %all-gather.16.cloned.1.call-start = ((), (), s32[]{:S(2)}) async-start(), calls=%async_computation.13 | async-start | bytes 10485760 | tf_op jit(solution)/shard_map/all_gather | solution.py:229
  333.7 410.7 %reduce-scatter.11.cloned.1.call-start = ((), (), s32[]{:S(2)}) async-start(), calls=%async_computation.11 | async-start | bytes 2621440 | tf_op jit(solution)/shard_map/reduce_scatter | solution.py:309
  401.5 345.0 %all-gather.20.cloned.1.call-start = ((), (), s32[]{:S(2)}) async-start(), calls=%async_computation.15 | async-start | bytes 10485760 | tf_op jit(solution)/shard_map/all_gather | solution.py:229
  504.9 147.3 %collective-permute-start = (bf16[4,256,512]{2,1,0:T(8,128)(2,1)}, bf16[4,256,512]{2,1,0:T(8,128)(2,1)}, u32[]{:S(2)}, u32[]{:S(2)}) collective-permute-start(bf16[4,256,512]{2,1,0:T(8,128)(2,1)} %bitcast.299), channel_id=1, source_target_pairs={{0,4},{4,0},{8,12},{12,8},{16,20},{20,16},{24,28},{28,24},{1,5},{5... | collective-permute-start | bytes 3145736 | tf_op jit(solution)/shard_map/ppermute | solution.py:115
  526.2 131.7 %collective-permute-start.4 = (bf16[4,256,512]{2,1,0:T(8,128)(2,1)}, bf16[4,256,512]{2,1,0:T(8,128)(2,1)}, u32[]{:S(2)}, u32[]{:S(2)}) collective-permute-start(bf16[4,256,512]{2,1,0:T(8,128)(2,1)} %bitcast.298), channel_id=1, source_target_pairs={{0,4},{4,0},{8,12},{12,8},{16,20},{20,16},{24,28},{28,24},{1,5},{5... | collective-permute-start | bytes 3145736 | tf_op jit(solution)/shard_map/ppermute | solution.py:115
  546.3 113.4 %collective-permute-start.8 = (bf16[4,256,512]{2,1,0:T(8,128)(2,1)}, bf16[4,256,512]{2,1,0:T(8,128)(2,1)}, u32[]{:S(2)}, u32[]{:S(2)}) collective-permute-start(bf16[4,256,512]{2,1,0:T(8,128)(2,1)} %bitcast.297), channel_id=1, source_target_pairs={{0,4},{4,0},{8,12},{12,8},{16,20},{20,16},{24,28},{28,24},{1,5},{5... | collective-permute-start | bytes 3145736 | tf_op jit(solution)/shard_map/ppermute | solution.py:115
  552.8 108.9 %collective-permute-start.12 = (bf16[4,512,256]{2,1,0:T(8,128)(2,1)}, bf16[4,512,256]{2,1,0:T(8,128)(2,1)}, u32[]{:S(2)}, u32[]{:S(2)}) collective-permute-start(bf16[4,512,256]{2,1,0:T(8,128)(2,1)} %fusion.56), channel_id=1, source_target_pairs={{0,4},{4,0},{8,12},{12,8},{16,20},{20,16},{24,28},{28,24},{1,5},{5... | collective-permute-start | bytes 3145736 | tf_op jit(solution)/shard_map/ppermute | solution.py:115
  659.7 46.1 %collective-permute-start.7 = (bf16[256,512]{1,0:T(8,128)(2,1)S(1)}, bf16[256,512]{1,0:T(8,128)(2,1)S(1)}, u32[]{:S(2)}, u32[]{:S(2)}) collective-permute-start(bf16[256,512]{1,0:T(8,128)(2,1)S(1)} %get-tuple-element.66), channel_id=1, source_target_pairs={{0,24},{4,28},{8,16},{12,20},{16,8},{20,12},{24,0},{28,4},{1,25},{... | collective-permute-start | bytes 786440 | tf_op jit(solution)/shard_map/ppermute | solution.py:115
  661.7 48.0 %collective-permute-start.6 = (bf16[256,512]{1,0:T(8,128)(2,1)S(1)}, bf16[256,512]{1,0:T(8,128)(2,1)S(1)}, u32[]{:S(2)}, u32[]{:S(2)}) collective-permute-start(bf16[256,512]{1,0:T(8,128)(2,1)S(1)} %get-tuple-element.67), channel_id=1, source_target_pairs={{0,16},{4,20},{8,24},{12,28},{16,0},{20,4},{24,8},{28,12},{1,17},{... | collective-permute-start | bytes 786440 | tf_op jit(solution)/shard_map/ppermute | solution.py:115
  671.9 38.9 %collective-permute-start.5 = (bf16[256,512]{1,0:T(8,128)(2,1)S(1)}, bf16[256,512]{1,0:T(8,128)(2,1)S(1)}, u32[]{:S(2)}, u32[]{:S(2)}) collective-permute-start(bf16[256,512]{1,0:T(8,128)(2,1)S(1)} %get-tuple-element.65), channel_id=1, source_target_pairs={{0,8},{4,12},{8,0},{12,4},{16,24},{20,28},{24,16},{28,20},{1,9},{5... | collective-permute-start | bytes 786440 | tf_op jit(solution)/shard_map/ppermute | solution.py:115
  686.5 41.9 %collective-permute-start.11 = (bf16[256,512]{1,0:T(8,128)(2,1)S(1)}, bf16[256,512]{1,0:T(8,128)(2,1)S(1)}, u32[]{:S(2)}, u32[]{:S(2)}) collective-permute-start(bf16[256,512]{1,0:T(8,128)(2,1)S(1)} %get-tuple-element.63), channel_id=1, source_target_pairs={{0,24},{4,28},{8,16},{12,20},{16,8},{20,12},{24,0},{28,4},{1,25},{... | collective-permute-start | bytes 786440 | tf_op jit(solution)/shard_map/ppermute | solution.py:115
  687.6 44.6 %collective-permute-start.10 = (bf16[256,512]{1,0:T(8,128)(2,1)S(1)}, bf16[256,512]{1,0:T(8,128)(2,1)S(1)}, u32[]{:S(2)}, u32[]{:S(2)}) collective-permute-start(bf16[256,512]{1,0:T(8,128)(2,1)S(1)} %get-tuple-element.64), channel_id=1, source_target_pairs={{0,16},{4,20},{8,24},{12,28},{16,0},{20,4},{24,8},{28,12},{1,17},{... | collective-permute-start | bytes 786440 | tf_op jit(solution)/shard_map/ppermute | solution.py:115
  763.0 36.9 %collective-permute-start.16 = (bf16[4,256,512]{2,1,0:T(8,128)(2,1)}, bf16[4,256,512]{2,1,0:T(8,128)(2,1)}, u32[]{:S(2)}, u32[]{:S(2)}) collective-permute-start(bf16[4,256,512]{2,1,0:T(8,128)(2,1)} %fusion.58), channel_id=1, source_target_pairs={{0,4},{4,0},{8,12},{12,8},{16,20},{20,16},{24,28},{28,24},{1,5},{5... | collective-permute-start | bytes 3145736 | tf_op jit(solution)/shard_map/ppermute | solution.py:115
  834.2 34.2 %collective-permute-start.23 = (bf16[256,512]{1,0:T(8,128)(2,1)S(1)}, bf16[256,512]{1,0:T(8,128)(2,1)S(1)}, u32[]{:S(2)}, u32[]{:S(2)}) collective-permute-start(bf16[256,512]{1,0:T(8,128)(2,1)S(1)} %get-tuple-element.47), channel_id=1, source_target_pairs={{0,24},{4,28},{8,16},{12,20},{16,8},{20,12},{24,0},{28,4},{1,25},{... | collective-permute-start | bytes 786440 | tf_op jit(solution)/shard_map/ppermute | solution.py:115
  835.6 37.3 %collective-permute-start.26 = (bf16[512,256]{1,0:T(8,128)(2,1)S(1)}, bf16[512,256]{1,0:T(8,128)(2,1)S(1)}, u32[]{:S(2)}, u32[]{:S(2)}) collective-permute-start(bf16[512,256]{1,0:T(8,128)(2,1)S(1)} %get-tuple-element.40), channel_id=1, source_target_pairs={{0,16},{4,20},{8,24},{12,28},{16,0},{20,4},{24,8},{28,12},{1,17},{... | collective-permute-start | bytes 786440 | tf_op jit(solution)/shard_map/ppermute | solution.py:115
  837.2 42.5 %collective-permute-start.27 = (bf16[512,256]{1,0:T(8,128)(2,1)S(1)}, bf16[512,256]{1,0:T(8,128)(2,1)S(1)}, u32[]{:S(2)}, u32[]{:S(2)}) collective-permute-start(bf16[512,256]{1,0:T(8,128)(2,1)S(1)} %get-tuple-element.39), channel_id=1, source_target_pairs={{0,24},{4,28},{8,16},{12,20},{16,8},{20,12},{24,0},{28,4},{1,25},{... | collective-permute-start | bytes 786440 | tf_op jit(solution)/shard_map/ppermute | solution.py:115
  (76 other events, 1115.2 us)
Sparse Core Ops, SparseCore 0:
  80.0 32.3 reduce-scatter.4
  115.9 22.9 all-gather.7
  164.0 31.0 reduce-scatter.6
  200.2 22.9 all-gather.9
  256.4 31.0 reduce-scatter.8
  289.5 44.0 all-gather.13
  335.9 23.5 all-gather.11
  361.7 43.6 all-gather.17
  407.0 59.2 all-gather.15
  469.5 30.9 reduce-scatter.10
  502.1 58.7 all-gather.19
